TPU v7x, 32 devices: a whole 2x2x4 slice. The times are simulated.
32 devices in a mesh: groups: 2 (over y), patch: 8 (over z, x), heads: 2 (over core).
Axes of the slice: x: 2, y: 2, z: 4, core: 2. Of those that a mesh axis runs over, the one named last changes fastest.
Arguments:
- hidden_in: bfloat16 [512, 1280], P(('groups', 'patch'), 'heads'), parts along dimension 0, may hold values from -150 to 150
- gn_gain: float32 [1280], P('heads'), may hold values from 0.25 to 1.75
- gn_bias: float32 [1280], P('heads'), may hold values from -3 to 3
- w_in: bfloat16 [1280, 1280], P(None, 'heads'), may hold values from -0.15625 to 0.15625
- b_in: float32 [1280], P('heads'), may hold values from -3 to 3
- ln_gain: float32 [1280], replicated, may hold values from 0.25 to 1.75
- ln_bias: float32 [1280], replicated, may hold values from -3 to 3
- w_qkv: bfloat16 [3, 1280, 1280], P(None, None, 'heads'), may hold values from -0.15625 to 0.15625
- stale_kv: bfloat16 [2, 512, 1280], P(None, ('groups', 'patch'), 'heads'), parts along dimension 1, may hold values from -64 to 64
- w_out: bfloat16 [1280, 1280], P('heads'), may hold values from -0.15625 to 0.15625
- b_out: float32 [1280], P('heads'), may hold values from -3 to 3
Outputs:
- hidden_out: float32 [512, 1280], P(('groups', 'patch'), 'heads'), parts along dimension 0
There are 2 independent parts, one for each index of `groups`. A program takes and returns all parts, laid end to end along the dimension named above; an argument that names none is the same for every part. Nothing has to cross between parts.
All inputs are finite; a program needn't handle non-finite values.
Results may differ from a plain program's by a relative error of at most 0.035.
Values may be sent and summed in bfloat16 or wider, within the bound.
No kernel may reach another device: no remote copies, remote signals or barrier semaphores. Data moves between devices by JAX's collectives and lax.ppermute only.
A program may use at most 128 MiB of HBM per device.

v0:
```python
import functools

import jax
import jax.numpy as jnp
from jax import lax
from jax.experimental import pallas as pl
from jax.experimental.pallas import tpu as pltpu
from jax.sharding import PartitionSpec as P


HD = 64
GROUPS = 32
STAT_ROWS = 16
COVER = 10_000_000_000
VMEM = pltpu.VMEM
BF = jnp.bfloat16
F32 = jnp.float32


def call(kernel, out_shape, n_in, scratch=(), spaces=None, flops=0, extra=0):
    return pl.pallas_call(
        kernel,
        out_shape=out_shape,
        in_specs=[pl.BlockSpec(memory_space=(spaces or {}).get(i, VMEM)) for i in range(n_in)],
        out_specs=jax.tree.map(lambda _: pl.BlockSpec(memory_space=VMEM), out_shape),
        scratch_shapes=list(scratch),
        cost_estimate=pl.CostEstimate(flops=flops, bytes_accessed=1 << 17, transcendentals=0),
        compiler_params=pltpu.CompilerParams(vmem_limit_bytes=(8 << 20) + extra),
    )


def sds(shape, dtype):
    return jax.ShapeDtypeStruct(shape, dtype)


def split3(x):
    hi = x.astype(BF)
    rest = x - hi.astype(F32)
    mid = rest.astype(BF)
    lo = (rest - mid.astype(F32)).astype(BF)
    return [hi.astype(F32), mid.astype(F32), lo.astype(F32)]


def col_stats(x):
    mean = jnp.mean(x, axis=0, keepdims=True)
    cen = x - mean
    return mean, jnp.sum(cen * cen, axis=0, keepdims=True)


def tick_kernel(out_ref):
    out_ref[...] = jnp.zeros_like(out_ref)


def stats_kernel(own_ref, other_ref, kv_ref, gain_ref, bias_ref, tick_ref, msg_ref, gb_ref):
    tok, width = own_ref.shape
    msg_ref[0 : 2 * tok, :] = kv_ref[...]
    rows = []
    for ref in (own_ref, other_ref):
        mean, m2 = col_stats(ref[...].astype(F32))
        rows += split3(mean) + split3(m2)
    rows.append(jnp.zeros((STAT_ROWS - len(rows), width), F32))
    msg_ref[2 * tok :, :] = jnp.concatenate(rows, axis=0).astype(BF)
    gb_ref[0:1, :] = gain_ref[...].reshape(1, width)
    gb_ref[1:2, :] = bias_ref[...].reshape(1, width)


def read_stats(msg_ref, base):
    s = msg_ref[base : base + STAT_ROWS, :].astype(F32)
    parts = [s[3 * i : 3 * i + 1] + s[3 * i + 1 : 3 * i + 2] + s[3 * i + 2 : 3 * i + 3] for i in range(4)]
    return parts


def merge_stats(parts, count):
    mean = parts[0][0]
    for p in parts[1:]:
        mean = mean + p[0]
    mean = mean * (1.0 / len(parts))
    m2 = None
    for p in parts:
        dev = p[0] - mean
        term = p[1] + count * (dev * dev)
        m2 = term if m2 is None else m2 + term
    return mean, m2


def merge_kernel(tok, *refs):
    msgs, (stat_ref, kv_ref) = refs[:-2], refs[-2:]
    all_parts = [read_stats(m, 2 * tok) for m in msgs]
    out = []
    for half in (0, 1):
        out += list(merge_stats([(p[2 * half], p[2 * half + 1]) for p in all_parts], float(tok)))
    out.append(jnp.zeros((8 - len(out), out[0].shape[1]), F32))
    stat_ref[...] = jnp.concatenate(out, axis=0)
    for i, m in enumerate(msgs[1:3]):
        kv_ref[2 * tok * i : 2 * tok * (i + 1), :] = m[0 : 2 * tok, :]


def in_kernel(count, group_size, h_ref, st_a, st_b, own_ref, other_ref, gb_ref, gb2_ref, b_ref, w_ref, out_ref):
    width = own_ref.shape[1]
    n_groups = width // group_size
    a, b = st_a[...], st_b[...]
    chan = lax.broadcasted_iota(jnp.int32, (n_groups, width), 1)
    grp = lax.broadcasted_iota(jnp.int32, (n_groups, width), 0) * group_size
    hot = jnp.where((chan >= grp) & (chan < grp + group_size), 1.0, 0.0)

    def over_group(row):
        per = jnp.sum(hot * row, axis=1, keepdims=True)
        return jnp.sum(hot * per, axis=0, keepdims=True)

    h = h_ref[0]
    acc = b_ref[...].reshape(1, width)
    for half, (x_ref, g_ref) in enumerate(((own_ref, gb_ref), (other_ref, gb2_ref))):
        mean, m2 = merge_stats(
            [(a[2 * half : 2 * half + 1], a[2 * half + 1 : 2 * half + 2]), (b[2 * half : 2 * half + 1], b[2 * half + 1 : 2 * half + 2])],
            count,
        )
        g_mean = over_group(mean) * (1.0 / group_size)
        dev = mean - g_mean
        var = over_group(m2 + (2.0 * count) * (dev * dev)) * (1.0 / (2.0 * count * group_size))
        scale = lax.rsqrt(var + 1e-06) * g_ref[0:1, :]
        normed = ((x_ref[...].astype(F32) - g_mean) * scale + g_ref[1:2, :]).astype(BF)
        first = pl.multiple_of((h if half == 0 else 1 - h) * width, 128)
        acc = acc + jnp.dot(normed, w_ref[pl.ds(first, width), :], preferred_element_type=F32)
    out_ref[...] = acc.astype(BF)


def qkv_kernel(h_ref, own_ref, other_ref, gain_ref, bias_ref, w_ref, out_ref):
    _, width = own_ref.shape
    full = 2 * width
    x = [own_ref[...].astype(F32), other_ref[...].astype(F32)]
    mean = (jnp.sum(x[0], axis=1, keepdims=True) + jnp.sum(x[1], axis=1, keepdims=True)) / full
    x = [v - mean for v in x]
    var = (jnp.sum(x[0] * x[0], axis=1, keepdims=True) + jnp.sum(x[1] * x[1], axis=1, keepdims=True)) / full
    rstd = lax.rsqrt(var + 1e-05)
    h = h_ref[0]
    firsts = [pl.multiple_of(h * width, 128), pl.multiple_of((1 - h) * width, 128)]
    gain, bias = ([r[pl.ds(f, width)].reshape(1, width) for f in firsts] for r in (gain_ref, bias_ref))
    normed = [(v * rstd * g + b).astype(BF) for v, g, b in zip(x, gain, bias)]
    for i in range(3):
        acc = jnp.dot(normed[0], w_ref[i, pl.ds(firsts[0], width), :], preferred_element_type=F32)
        acc = acc + jnp.dot(normed[1], w_ref[i, pl.ds(firsts[1], width), :], preferred_element_type=F32)
        out_ref[i] = acc.astype(BF)


def attn_kernel(sources, h_ref, qkv_ref, *refs):
    n_src = max((s[0] for s in sources), default=-1) + 1
    srcs, w_ref, att_ref, send_ref, k_scr, v_scr = refs[:n_src], *refs[n_src:]
    tok, width = qkv_ref.shape[1:]
    at = 0
    if len(srcs) == 0 or sources[0][4]:
        k_scr[0:tok, :] = qkv_ref[1]
        v_scr[0:tok, :] = qkv_ref[2]
        at = tok
    for i, k0, v0, rows, _ in sources:
        k_scr[at : at + rows, :] = srcs[i][k0 : k0 + rows, :]
        v_scr[at : at + rows, :] = srcs[i][v0 : v0 + rows, :]
        at += rows
    pair = 2 * HD
    low = lax.broadcasted_iota(jnp.int32, (tok, pair), 1) < HD
    for p in range(width // pair):
        cols = slice(p * pair, (p + 1) * pair)
        q = qkv_ref[0, :, cols].astype(F32) * (HD ** (-0.5))
        q2 = jnp.concatenate([jnp.where(low, q, 0.0), jnp.where(low, 0.0, q)], axis=0).astype(BF)
        scores = lax.dot_general(q2, k_scr[:, cols], (((1,), (1,)), ((), ())), preferred_element_type=F32)
        top = jnp.max(scores, axis=1, keepdims=True)
        wts = jnp.exp(scores - top)
        total = jnp.sum(wts, axis=1, keepdims=True)
        out = jnp.dot(wts.astype(BF), v_scr[:, cols], preferred_element_type=F32) / total
        att_ref[:, cols] = jnp.where(low, out[0:tok], out[tok:]).astype(BF)
    first = pl.multiple_of((1 - h_ref[0]) * width, 128)
    send_ref[...] = jnp.dot(att_ref[...], w_ref[:, pl.ds(first, width)], preferred_element_type=F32)


def own_kernel(h_ref, att_ref, stream_ref, b_ref, w_ref, out_ref):
    width = stream_ref.shape[1]
    first = pl.multiple_of(h_ref[0] * width, 128)
    part = jnp.dot(att_ref[...], w_ref[:, pl.ds(first, width)], preferred_element_type=F32)
    out_ref[...] = part + stream_ref[...].astype(F32) + b_ref[...].reshape(1, width)


def body(hidden_in, gn_gain, gn_bias, w_in, b_in, ln_gain, ln_bias, w_qkv, stale_kv, w_out, b_out):
    tok, width = hidden_in.shape
    full = ln_gain.shape[0]
    group_size = full // GROUPS
    n = lax.axis_size("patch")
    swap = [(0, 1), (1, 0)]
    h = lax.axis_index("heads").astype(jnp.int32).reshape(1)
    smem = {0: pltpu.SMEM}

    kv_own = stale_kv.reshape(2 * tok, width)
    partner = lambda k: [(i, i ^ k) for i in range(n)]

    def move(x, k):
        return lax.ppermute(x, "patch", partner(k)) if k else lax.ppermute(x, "heads", swap)

    direct = n == 8
    if direct:
        strip_x = move(kv_own, 1)
    other = move(hidden_in, 0)
    tick = call(tick_kernel, sds((8, 128), F32), 0, flops=COVER)()
    msg, gb = call(
        stats_kernel, (sds((2 * tok + STAT_ROWS, width), BF), sds((2, width), F32)), 6, flops=COVER
    )(hidden_in, other, kv_own, gn_gain, gn_bias, tick)
    stat_out = sds((8, width), F32)
    if direct:
        z2, z3, z1 = move(msg, 4), move(msg, 6), move(msg, 2)
        strip_xz1 = move(kv_own, 3)
        gb_other = move(gb, 0)
        stat, kv2 = call(
            functools.partial(merge_kernel, tok), (stat_out, sds((2 * 2 * tok, width), BF)), 4, flops=COVER
        )(msg, z2, z3, z1)
        stat_x = move(stat, 1)
        strip_two = move(kv2, 1)
        count = float(tok * (n // 2))
        strips = [strip_x, z1, strip_xz1, kv2, strip_two]
        sources = [(i, 0, tok, tok, True) for i in range(3)]
        for i in (3, 4):
            sources += [(i, 2 * tok * j, 2 * tok * j + tok, tok, True) for j in range(2)]
    else:
        gb_other = move(gb, 0)
        rows = lax.all_gather(msg[2 * tok :], "patch").astype(F32)
        rows = rows[:, :12].reshape(n, 4, 3, width).sum(axis=2)
        means, m2s = rows[:, 0::2], rows[:, 1::2]
        mean = means.mean(axis=0)
        m2 = m2s.sum(axis=0) + float(tok) * ((means - mean[None]) ** 2).sum(axis=0)
        stat = jnp.concatenate([jnp.stack([mean[0], 0.5 * m2[0], mean[1], 0.5 * m2[1]]), jnp.zeros((4, width), F32)])
        stat_x = stat
        count = float(tok * n) / 2.0

    stream = call(
        functools.partial(in_kernel, count, group_size), sds((tok, width), BF), 9, spaces=smem, flops=COVER
    )(h, stat, stat_x, hidden_in, other, gb, gb_other, b_in, w_in)
    stream_other = move(stream, 0)
    qkv = call(qkv_kernel, sds((3, tok, width), BF), 6, spaces=smem, flops=COVER)(
        h, stream, stream_other, ln_gain, ln_bias, w_qkv
    )
    n_keys = n * tok
    if not direct:
        kv_all = lax.all_gather(stale_kv, "patch", axis=1, tiled=True)
        kv_all = lax.dynamic_update_slice(kv_all, qkv[1:], (0, lax.axis_index("patch") * tok, 0))
        strips = [kv_all.reshape(2 * n_keys, width)]
        sources = [(0, 0, n_keys, n_keys, False)]
    attended, send = call(
        functools.partial(attn_kernel, sources),
        (sds((tok, width), BF), sds((tok, width), F32)),
        3 + len(strips),
        scratch=[VMEM((n_keys, width), BF), VMEM((n_keys, width), BF)],
        extra=4 * n_keys * width + 16 * 2 * tok * n_keys,
        spaces=smem,
    )(h, qkv, *strips, w_out)
    received = move(send, 0)
    mine = call(own_kernel, sds((tok, width), F32), 5, spaces=smem)(h, attended, stream, b_out, w_out)
    return mine + received


def solution(mesh):
    placed = (
        P(("groups", "patch"), "heads"),
        P("heads"),
        P("heads"),
        P(None, "heads"),
        P("heads"),
        P(),
        P(),
        P(None, None, "heads"),
        P(None, ("groups", "patch"), "heads"),
        P("heads", None),
        P("heads"),
    )

    return jax.shard_map(body, mesh=mesh, in_specs=placed, out_specs=P(("groups", "patch"), "heads"), check_vma=False)
```

profile of v0, /device:TPU:0, one launch (start us, length us, event | category | flops | bytes accessed | tf_op | source)
XLA Modules:
  0.0 35.5 jit_solution(11523817806657630339)
XLA Ops:
  0.0 0.0 copy-start.5
  0.0 0.0 copy-start.4
  0.0 0.0 copy-start.9
  0.0 0.0 copy-start.8
  0.0 0.6 %collective-permute-start = (bf16[32,640]{1,0:T(8,128)(2,1)}, bf16[32,640]{1,0:T(8,128)(2,1)S(1)}, u32[]{:S(2)}, u32[]{:S(2)}) collective-permute-start(bf16[32,640]{1,0:T(8,128)(2,1)} %own_ref.3), channel_id=1, source_target_pairs={{0,1},{1,0},{2,3},{3,2},{4,5},{5,4},{6,7},{7,6},{8,9},{9,8},{10,11... | collective-permute-start | bytes 122888 | tf_op jit(solution)/shard_map/ppermute | solution.py:194
  0.6 1.1 %collective-permute-done.other_ref = bf16[32,640]{1,0:T(8,128)(2,1)S(1)} collective-permute-done((bf16[32,640]{1,0:T(8,128)(2,1)}, bf16[32,640]{1,0:T(8,128)(2,1)S(1)}, u32[]{:S(2)}, u32[]{:S(2)}) %collective-permute-start) | collective-permute-done | bytes 40992 | tf_op jit(solution)/shard_map/ppermute | solution.py:194
  1.7 0.0 copy-done.5
  1.7 0.0 copy-done.4
  1.7 0.0 copy-done.9
  1.7 0.0 copy-done.8
  1.7 0.1 shard_map.110
  1.8 0.0 copy-start.3
  1.8 0.0 copy-start.10
  1.8 3.0 %collective-permute-start.3 = (bf16[80,640]{1,0:T(8,128)(2,1)S(1)}, bf16[80,640]{1,0:T(8,128)(2,1)S(1)}, u32[]{:S(2)}, u32[]{:S(2)}) collective-permute-start(bf16[80,640]{1,0:T(8,128)(2,1)S(1)} %get-tuple-element.11.refs_0_), channel_id=1, source_target_pairs={{0,4},{2,6},{4,0},{6,2},{8,12},{10,14},{12,8},{14,10},{1,5},{3,7},... | collective-permute-start | bytes 307208 | tf_op jit(solution)/shard_map/ppermute | solution.py:194
  4.8 2.5 %collective-permute-start.2 = (bf16[80,640]{1,0:T(8,128)(2,1)S(1)}, bf16[80,640]{1,0:T(8,128)(2,1)S(1)}, u32[]{:S(2)}, u32[]{:S(2)}) collective-permute-start(bf16[80,640]{1,0:T(8,128)(2,1)S(1)} %get-tuple-element.11.refs_0_), channel_id=1, source_target_pairs={{0,12},{2,14},{4,8},{6,10},{8,4},{10,6},{12,0},{14,2},{1,13},{3,15... | collective-permute-start | bytes 307208 | tf_op jit(solution)/shard_map/ppermute | solution.py:194
  7.2 0.1 collective-permute-start.1
  7.4 0.6 %collective-permute-done.3.refs_3_.refs_1_ = bf16[80,640]{1,0:T(8,128)(2,1)S(1)} collective-permute-done((bf16[80,640]{1,0:T(8,128)(2,1)S(1)}, bf16[80,640]{1,0:T(8,128)(2,1)S(1)}, u32[]{:S(2)}, u32[]{:S(2)}) %collective-permute-start.3) | collective-permute-done | bytes 102432 | tf_op jit(solution)/shard_map/ppermute | solution.py:194
  8.0 5.3 %collective-permute-done.2.refs_2_ = bf16[80,640]{1,0:T(8,128)(2,1)S(1)} collective-permute-done((bf16[80,640]{1,0:T(8,128)(2,1)S(1)}, bf16[80,640]{1,0:T(8,128)(2,1)S(1)}, u32[]{:S(2)}, u32[]{:S(2)}) %collective-permute-start.2) | collective-permute-done | bytes 102432 | tf_op jit(solution)/shard_map/ppermute | solution.py:194
  13.3 3.6 %collective-permute-done.1.refs_1_ = bf16[80,640]{1,0:T(8,128)(2,1)S(1)} collective-permute-done((bf16[80,640]{1,0:T(8,128)(2,1)S(1)}, bf16[80,640]{1,0:T(8,128)(2,1)S(1)}, u32[]{:S(2)}, u32[]{:S(2)}) %collective-permute-start.1) | collective-permute-done | bytes 102432 | tf_op jit(solution)/shard_map/ppermute | solution.py:194
  16.9 0.1 shard_map.111
  16.9 1.6 %collective-permute-start.4 = (f32[8,640]{1,0:T(8,128)S(1)}, f32[8,640]{1,0:T(8,128)S(1)}, u32[]{:S(2)}, u32[]{:S(2)}) collective-permute-start(f32[8,640]{1,0:T(8,128)S(1)} %get-tuple-element.12.st_a), channel_id=1, source_target_pairs={{0,2},{2,0},{4,6},{6,4},{8,10},{10,8},{12,14},{14,12},{1,3},{3,1},... | collective-permute-start | bytes 61448 | tf_op jit(solution)/shard_map/ppermute | solution.py:194
  18.5 0.0 collective-permute-start.5
  18.5 1.2 %collective-permute-done.5.gb2_ref = f32[2,640]{1,0:T(2,128)S(1)} collective-permute-done((f32[2,640]{1,0:T(2,128)S(1)}, f32[2,640]{1,0:T(2,128)S(1)}, u32[]{:S(2)}, u32[]{:S(2)}) %collective-permute-start.5) | collective-permute-done | bytes 5152 | tf_op jit(solution)/shard_map/ppermute | solution.py:194
  19.7 1.1 %collective-permute-done.4.st_b = f32[8,640]{1,0:T(8,128)S(1)} collective-permute-done((f32[8,640]{1,0:T(8,128)S(1)}, f32[8,640]{1,0:T(8,128)S(1)}, u32[]{:S(2)}, u32[]{:S(2)}) %collective-permute-start.4) | collective-permute-done | bytes 20512 | tf_op jit(solution)/shard_map/ppermute | solution.py:194
  20.8 0.0 copy-done.3
  20.8 0.0 copy-done.10
  20.8 0.6 %shard_map.112.own_ref.stream_ref = bf16[32,640]{1,0:T(8,128)(2,1)S(1)} custom-call(s32[1]{0:T(128)} %bitcast.h_ref, f32[8,640]{1,0:T(8,128)S(1)} %get-tuple-element.12.st_a, f32[8,640]{1,0:T(8,128)S(1)} %collective-permute-done.4.st_b, bf16[32,640]{1,0:T(8,128)(2,1)S(1)} %copy-done.5, bf16[32,640]{1,0:T(8,128)(2,1)S(1)} %collective-permute-done.other_ref, ...), custom_call_target="tpu_custom_call" | custom-call | flops 10000000000 | bytes 131072 | tf_op jit(solution)/shard_map/pallas_call | solution.py:230
  21.4 0.1 collective-permute-start.6
  21.5 0.8 %collective-permute-start.8 = (bf16[64,640]{1,0:T(8,128)(2,1)S(1)}, bf16[64,640]{1,0:T(8,128)(2,1)S(1)}, u32[]{:S(2)}, u32[]{:S(2)}) collective-permute-start(bf16[64,640]{1,0:T(8,128)(2,1)S(1)} %bitcast.3), channel_id=1, source_target_pairs={{0,6},{2,4},{4,2},{6,0},{8,14},{10,12},{12,10},{14,8},{1,7},{3,5},... | collective-permute-start | bytes 245768 | tf_op jit(solution)/shard_map/ppermute | solution.py:194
  22.3 0.8 %collective-permute-start.7 = (bf16[64,640]{1,0:T(8,128)(2,1)S(1)}, bf16[64,640]{1,0:T(8,128)(2,1)S(1)}, u32[]{:S(2)}, u32[]{:S(2)}) collective-permute-start(bf16[64,640]{1,0:T(8,128)(2,1)S(1)} %bitcast.4), channel_id=1, source_target_pairs={{0,2},{2,0},{4,6},{6,4},{8,10},{10,8},{12,14},{14,12},{1,3},{3,1},... | collective-permute-start | bytes 245768 | tf_op jit(solution)/shard_map/ppermute | solution.py:194
  23.1 1.2 %collective-permute-start.9 = (bf16[128,640]{1,0:T(8,128)(2,1)S(1)}, bf16[128,640]{1,0:T(8,128)(2,1)S(1)}, u32[]{:S(2)}, u32[]{:S(2)}) collective-permute-start(bf16[128,640]{1,0:T(8,128)(2,1)S(1)} %get-tuple-element.14.refs_3_), channel_id=1, source_target_pairs={{0,2},{2,0},{4,6},{6,4},{8,10},{10,8},{12,14},{14,12},{1,3},{3,1},... | collective-permute-start | bytes 491528 | tf_op jit(solution)/shard_map/ppermute | solution.py:194
  24.3 0.0 collective-permute-done.6.other_ref
  24.3 0.0 copy-done.6
  24.3 0.0 copy-done.7
  24.3 0.0 copy-start.2
  24.3 2.4 %copy-done.2 = bf16[3,1280,640]{2,1,0:T(8,128)(2,1)S(1)} copy-done((bf16[3,1280,640]{2,1,0:T(8,128)(2,1)S(1)}, bf16[3,1280,640]{2,1,0:T(8,128)(2,1)}, u32[]{:S(2)}) %copy-start.2) | copy-done | bytes 4915224
  26.7 1.0 %shard_map.113.qkv_ref = bf16[3,32,640]{2,1,0:T(8,128)(2,1)S(1)} custom-call(s32[1]{0:T(128)} %bitcast.h_ref, bf16[32,640]{1,0:T(8,128)(2,1)S(1)} %shard_map.112.own_ref.stream_ref, bf16[32,640]{1,0:T(8,128)(2,1)S(1)} %collective-permute-done.6.other_ref, f32[1280]{0:T(1024)S(1)} %copy-done.6, f32[1280]{0:T(1024)S(1)} %copy-done.7, ...), custom_call_target="tpu_custom_call" | custom-call | flops 10000000000 | bytes 131072 | tf_op jit(solution)/shard_map/pallas_call | solution.py:234
  27.7 0.0 copy-start.1
  27.7 0.0 collective-permute-done.8.refs_2_
  27.7 1.3 %collective-permute-done.7.refs_0_ = bf16[64,640]{1,0:T(8,128)(2,1)S(1)} collective-permute-done((bf16[64,640]{1,0:T(8,128)(2,1)S(1)}, bf16[64,640]{1,0:T(8,128)(2,1)S(1)}, u32[]{:S(2)}, u32[]{:S(2)}) %collective-permute-start.7) | collective-permute-done | bytes 81952 | tf_op jit(solution)/shard_map/ppermute | solution.py:194
  29.1 3.0 %collective-permute-done.9.refs_4_ = bf16[128,640]{1,0:T(8,128)(2,1)S(1)} collective-permute-done((bf16[128,640]{1,0:T(8,128)(2,1)S(1)}, bf16[128,640]{1,0:T(8,128)(2,1)S(1)}, u32[]{:S(2)}, u32[]{:S(2)}) %collective-permute-start.9) | collective-permute-done | bytes 163872 | tf_op jit(solution)/shard_map/ppermute | solution.py:194
  32.0 0.0 copy-done
  32.0 1.5 %shard_map.114 = (bf16[32,640]{1,0:T(8,128)(2,1)S(1)}, f32[32,640]{1,0:T(8,128)S(1)}) custom-call(s32[1]{0:T(128)} %bitcast.h_ref, bf16[3,32,640]{2,1,0:T(8,128)(2,1)S(1)} %shard_map.113.qkv_ref, bf16[64,640]{1,0:T(8,128)(2,1)S(1)} %collective-permute-done.7.refs_0_, bf16[80,640]{1,0:T(8,128)(2,1)S(1)} %collective-permute-done.3.refs_3_.refs_1_, ...), custom_call_target="tpu_custom_call" | custom-call | bytes 131072 | tf_op jit(solution)/shard_map/pallas_call | solution.py:243
  33.5 0.1 collective-permute-start.10
  33.6 0.0 copy-done.1
  33.6 0.3 shard_map.115
  33.9 1.0 %collective-permute-done.10 = f32[32,640]{1,0:T(8,128)S(1)} collective-permute-done((f32[32,640]{1,0:T(8,128)S(1)}, f32[32,640]{1,0:T(8,128)S(1)}, u32[]{:S(2)}, u32[]{:S(2)}) %collective-permute-start.10) | collective-permute-done | bytes 81952 | tf_op jit(solution)/shard_map/ppermute | solution.py:194
  34.9 0.6 %add.3 = f32[32,640]{1,0:T(8,128)} add(f32[32,640]{1,0:T(8,128)S(1)} %shard_map.115, f32[32,640]{1,0:T(8,128)S(1)} %collective-permute-done.10) | non-fusion elementwise | flops 20480 | bytes 245760 | tf_op jit(solution)/shard_map/add | solution.py:253
  (4 shorter events, 0.0 us)
Async XLA Ops:
  0.0 1.7 %copy-start.5 = (bf16[32,640]{1,0:T(8,128)(2,1)S(1)}, bf16[32,640]{1,0:T(8,128)(2,1)}, u32[]{:S(2)}) copy-start(bf16[32,640]{1,0:T(8,128)(2,1)} %own_ref.3) | copy-start | bytes 122884
  0.0 1.7 %copy-start.4 = (bf16[2,32,640]{2,1,0:T(8,128)(2,1)S(1)}, bf16[2,32,640]{2,1,0:T(8,128)(2,1)}, u32[]{:S(2)}) copy-start(bf16[2,32,640]{2,1,0:T(8,128)(2,1)} %param.19) | copy-start | bytes 245764
  0.0 1.7 %copy-start.9 = (f32[640]{0:T(1024)S(1)}, f32[640]{0:T(1024)}, u32[]{:S(2)}) copy-start(f32[640]{0:T(1024)} %bias_ref.2) | copy-start | bytes 7684
  0.0 1.7 %copy-start.8 = (f32[640]{0:T(1024)S(1)}, f32[640]{0:T(1024)}, u32[]{:S(2)}) copy-start(f32[640]{0:T(1024)} %gain_ref.2) | copy-start | bytes 7684
  0.0 1.6 %collective-permute-start = (bf16[32,640]{1,0:T(8,128)(2,1)}, bf16[32,640]{1,0:T(8,128)(2,1)S(1)}, u32[]{:S(2)}, u32[]{:S(2)}) collective-permute-start(bf16[32,640]{1,0:T(8,128)(2,1)} %own_ref.3), channel_id=1, source_target_pairs={{0,1},{1,0},{2,3},{3,2},{4,5},{5,4},{6,7},{7,6},{8,9},{9,8},{10,11... | collective-permute-start | bytes 122888 | tf_op jit(solution)/shard_map/ppermute | solution.py:194
  1.8 19.0 %copy-start.3 = (bf16[1280,640]{1,0:T(8,128)(2,1)S(1)}, bf16[1280,640]{1,0:T(8,128)(2,1)}, u32[]{:S(2)}) copy-start(bf16[1280,640]{1,0:T(8,128)(2,1)} %w_ref.3) | copy-start | bytes 4915204
  1.8 19.0 %copy-start.10 = (f32[640]{0:T(1024)S(1)}, f32[640]{0:T(1024)}, u32[]{:S(2)}) copy-start(f32[640]{0:T(1024)} %b_ref.2) | copy-start | bytes 7684
  1.8 6.2 %collective-permute-start.3 = (bf16[80,640]{1,0:T(8,128)(2,1)S(1)}, bf16[80,640]{1,0:T(8,128)(2,1)S(1)}, u32[]{:S(2)}, u32[]{:S(2)}) collective-permute-start(bf16[80,640]{1,0:T(8,128)(2,1)S(1)} %get-tuple-element.11.refs_0_), channel_id=1, source_target_pairs={{0,4},{2,6},{4,0},{6,2},{8,12},{10,14},{12,8},{14,10},{1,5},{3,7},... | collective-permute-start | bytes 307208 | tf_op jit(solution)/shard_map/ppermute | solution.py:194
  4.8 8.5 %collective-permute-start.2 = (bf16[80,640]{1,0:T(8,128)(2,1)S(1)}, bf16[80,640]{1,0:T(8,128)(2,1)S(1)}, u32[]{:S(2)}, u32[]{:S(2)}) collective-permute-start(bf16[80,640]{1,0:T(8,128)(2,1)S(1)} %get-tuple-element.11.refs_0_), channel_id=1, source_target_pairs={{0,12},{2,14},{4,8},{6,10},{8,4},{10,6},{12,0},{14,2},{1,13},{3,15... | collective-permute-start | bytes 307208 | tf_op jit(solution)/shard_map/ppermute | solution.py:194
  7.2 9.6 %collective-permute-start.1 = (bf16[80,640]{1,0:T(8,128)(2,1)S(1)}, bf16[80,640]{1,0:T(8,128)(2,1)S(1)}, u32[]{:S(2)}, u32[]{:S(2)}) collective-permute-start(bf16[80,640]{1,0:T(8,128)(2,1)S(1)} %get-tuple-element.11.refs_0_), channel_id=1, source_target_pairs={{0,8},{2,10},{4,12},{6,14},{8,0},{10,2},{12,4},{14,6},{1,9},{3,11}... | collective-permute-start | bytes 307208 | tf_op jit(solution)/shard_map/ppermute | solution.py:194
  16.9 3.8 %collective-permute-start.4 = (f32[8,640]{1,0:T(8,128)S(1)}, f32[8,640]{1,0:T(8,128)S(1)}, u32[]{:S(2)}, u32[]{:S(2)}) collective-permute-start(f32[8,640]{1,0:T(8,128)S(1)} %get-tuple-element.12.st_a), channel_id=1, source_target_pairs={{0,2},{2,0},{4,6},{6,4},{8,10},{10,8},{12,14},{14,12},{1,3},{3,1},... | collective-permute-start | bytes 61448 | tf_op jit(solution)/shard_map/ppermute | solution.py:194
  18.5 1.2 %collective-permute-start.5 = (f32[2,640]{1,0:T(2,128)S(1)}, f32[2,640]{1,0:T(2,128)S(1)}, u32[]{:S(2)}, u32[]{:S(2)}) collective-permute-start(f32[2,640]{1,0:T(2,128)S(1)} %get-tuple-element.13.gb_ref), channel_id=1, source_target_pairs={{0,1},{1,0},{2,3},{3,2},{4,5},{5,4},{6,7},{7,6},{8,9},{9,8},{10,11... | collective-permute-start | bytes 15368 | tf_op jit(solution)/shard_map/ppermute | solution.py:194
  20.8 3.5 %copy-start.6 = (f32[1280]{0:T(1024)S(1)}, f32[1280]{0:T(1024)}, u32[]{:S(2)}) copy-start(f32[1280]{0:T(1024)} %gain_ref.3) | copy-start | bytes 15364
  20.8 3.5 %copy-start.7 = (f32[1280]{0:T(1024)S(1)}, f32[1280]{0:T(1024)}, u32[]{:S(2)}) copy-start(f32[1280]{0:T(1024)} %bias_ref.3) | copy-start | bytes 15364
  21.4 2.9 %collective-permute-start.6 = (bf16[32,640]{1,0:T(8,128)(2,1)S(1)}, bf16[32,640]{1,0:T(8,128)(2,1)S(1)}, u32[]{:S(2)}, u32[]{:S(2)}) collective-permute-start(bf16[32,640]{1,0:T(8,128)(2,1)S(1)} %shard_map.112.own_ref.stream_ref), channel_id=1, source_target_pairs={{0,1},{1,0},{2,3},{3,2},{4,5},{5,4},{6,7},{7,6},{8,9},{9,8},{10,11... | collective-permute-start | bytes 122888 | tf_op jit(solution)/shard_map/ppermute | solution.py:194
  21.5 6.3 %collective-permute-start.8 = (bf16[64,640]{1,0:T(8,128)(2,1)S(1)}, bf16[64,640]{1,0:T(8,128)(2,1)S(1)}, u32[]{:S(2)}, u32[]{:S(2)}) collective-permute-start(bf16[64,640]{1,0:T(8,128)(2,1)S(1)} %bitcast.3), channel_id=1, source_target_pairs={{0,6},{2,4},{4,2},{6,0},{8,14},{10,12},{12,10},{14,8},{1,7},{3,5},... | collective-permute-start | bytes 245768 | tf_op jit(solution)/shard_map/ppermute | solution.py:194
  22.3 6.8 %collective-permute-start.7 = (bf16[64,640]{1,0:T(8,128)(2,1)S(1)}, bf16[64,640]{1,0:T(8,128)(2,1)S(1)}, u32[]{:S(2)}, u32[]{:S(2)}) collective-permute-start(bf16[64,640]{1,0:T(8,128)(2,1)S(1)} %bitcast.4), channel_id=1, source_target_pairs={{0,2},{2,0},{4,6},{6,4},{8,10},{10,8},{12,14},{14,12},{1,3},{3,1},... | collective-permute-start | bytes 245768 | tf_op jit(solution)/shard_map/ppermute | solution.py:194
  23.1 9.0 %copy-start = (bf16[640,1280]{1,0:T(8,128)(2,1)S(1)}, bf16[640,1280]{1,0:T(8,128)(2,1)}, u32[]{:S(2)}) copy-start(bf16[640,1280]{1,0:T(8,128)(2,1)} %w_ref.5) | copy-start | bytes 4915204
  23.1 8.9 %collective-permute-start.9 = (bf16[128,640]{1,0:T(8,128)(2,1)S(1)}, bf16[128,640]{1,0:T(8,128)(2,1)S(1)}, u32[]{:S(2)}, u32[]{:S(2)}) collective-permute-start(bf16[128,640]{1,0:T(8,128)(2,1)S(1)} %get-tuple-element.14.refs_3_), channel_id=1, source_target_pairs={{0,2},{2,0},{4,6},{6,4},{8,10},{10,8},{12,14},{14,12},{1,3},{3,1},... | collective-permute-start | bytes 491528 | tf_op jit(solution)/shard_map/ppermute | solution.py:194
  24.3 2.4 %copy-start.2 = (bf16[3,1280,640]{2,1,0:T(8,128)(2,1)S(1)}, bf16[3,1280,640]{2,1,0:T(8,128)(2,1)}, u32[]{:S(2)}) copy-start(bf16[3,1280,640]{2,1,0:T(8,128)(2,1)} %w_ref.4) | copy-start | bytes 14745604
  27.7 5.9 %copy-start.1 = (f32[640]{0:T(1024)S(1)}, f32[640]{0:T(1024)}, u32[]{:S(2)}) copy-start(f32[640]{0:T(1024)} %b_ref.3) | copy-start | bytes 7684
  33.5 1.3 %collective-permute-start.10 = (f32[32,640]{1,0:T(8,128)S(1)}, f32[32,640]{1,0:T(8,128)S(1)}, u32[]{:S(2)}, u32[]{:S(2)}) collective-permute-start(f32[32,640]{1,0:T(8,128)S(1)} %get-tuple-element.16), channel_id=1, source_target_pairs={{0,1},{1,0},{2,3},{3,2},{4,5},{5,4},{6,7},{7,6},{8,9},{9,8},{10,11... | collective-permute-start | bytes 245768 | tf_op jit(solution)/shard_map/ppermute | solution.py:194
where the time goes:
time: 35.7 us; the launch traced here: 35.5 us
  waiting for transfers between devices  18.2 us (51%)
  starting transfers between devices  10.7 us (30%)
  Pallas kernels  3.48 us (10%)
  local copies, waits for them, and re-layouts  2.43 us (7%)
  other arithmetic  0.65 us (2%)
    ppermute x7, waiting for transfers between devices, move(): lax.ppermute(x, 'patch', partner(k))  14.9 us
    ppermute x7, starting transfers between devices, move(): lax.ppermute(x, 'patch', partner(k))  9.97 us
    ppermute x4, waiting for transfers between devices, move(): lax.ppermute(x, 'heads', swap)  3.24 us
    unnamed x22, local copies, waits for them, and re-layouts  2.43 us
    pallas_call x1, Pallas kernels, body(): call(functools.partial(attn_kernel, sources), (sds((tok, width), BF), sds...  1.49 us
    pallas_call x1, Pallas kernels, body(): call(qkv_kernel, sds((3, tok, width), BF), 6, spaces=smem, flops=COVER)  0.99 us
  transfers between devices with their start and end apart: 11, of which 9 were waited for; matrix products, arithmetic and copies ran while one was open for 0% of the time, Pallas kernels for 4%

commit v1 on v0

--- a/solution.py
+++ b/solution.py
@@ -95,7 +95,7 @@
         kv_ref[2 * tok * i : 2 * tok * (i + 1), :] = m[0 : 2 * tok, :]
 
 
-def in_kernel(count, group_size, h_ref, st_a, st_b, own_ref, other_ref, gb_ref, gb2_ref, b_ref, w_ref, out_ref):
+def in_kernel(count, group_size, st_a, st_b, own_ref, other_ref, gb_ref, gb2_ref, b_ref, w_ref, out_ref):
     width = own_ref.shape[1]
     n_groups = width // group_size
     a, b = st_a[...], st_b[...]
@@ -107,7 +107,7 @@
         per = jnp.sum(hot * row, axis=1, keepdims=True)
         return jnp.sum(hot * per, axis=0, keepdims=True)
 
-    h = h_ref[0]
+    h = lax.axis_index("heads")
     acc = b_ref[...].reshape(1, width)
     for half, (x_ref, g_ref) in enumerate(((own_ref, gb_ref), (other_ref, gb2_ref))):
         mean, m2 = merge_stats(
@@ -124,7 +124,7 @@
     out_ref[...] = acc.astype(BF)
 
 
-def qkv_kernel(h_ref, own_ref, other_ref, gain_ref, bias_ref, w_ref, out_ref):
+def qkv_kernel(own_ref, other_ref, gain_ref, bias_ref, w_ref, out_ref):
     _, width = own_ref.shape
     full = 2 * width
     x = [own_ref[...].astype(F32), other_ref[...].astype(F32)]
@@ -132,7 +132,7 @@
     x = [v - mean for v in x]
     var = (jnp.sum(x[0] * x[0], axis=1, keepdims=True) + jnp.sum(x[1] * x[1], axis=1, keepdims=True)) / full
     rstd = lax.rsqrt(var + 1e-05)
-    h = h_ref[0]
+    h = lax.axis_index("heads")
     firsts = [pl.multiple_of(h * width, 128), pl.multiple_of((1 - h) * width, 128)]
     gain, bias = ([r[pl.ds(f, width)].reshape(1, width) for f in firsts] for r in (gain_ref, bias_ref))
     normed = [(v * rstd * g + b).astype(BF) for v, g, b in zip(x, gain, bias)]
@@ -142,7 +142,7 @@
         out_ref[i] = acc.astype(BF)
 
 
-def attn_kernel(sources, h_ref, qkv_ref, *refs):
+def attn_kernel(sources, qkv_ref, *refs):
     n_src = max((s[0] for s in sources), default=-1) + 1
     srcs, w_ref, att_ref, send_ref, k_scr, v_scr = refs[:n_src], *refs[n_src:]
     tok, width = qkv_ref.shape[1:]
@@ -167,13 +167,13 @@
         total = jnp.sum(wts, axis=1, keepdims=True)
         out = jnp.dot(wts.astype(BF), v_scr[:, cols], preferred_element_type=F32) / total
         att_ref[:, cols] = jnp.where(low, out[0:tok], out[tok:]).astype(BF)
-    first = pl.multiple_of((1 - h_ref[0]) * width, 128)
+    first = pl.multiple_of((1 - lax.axis_index("heads")) * width, 128)
     send_ref[...] = jnp.dot(att_ref[...], w_ref[:, pl.ds(first, width)], preferred_element_type=F32)
 
 
-def own_kernel(h_ref, att_ref, stream_ref, b_ref, w_ref, out_ref):
+def own_kernel(att_ref, stream_ref, b_ref, w_ref, out_ref):
     width = stream_ref.shape[1]
-    first = pl.multiple_of(h_ref[0] * width, 128)
+    first = pl.multiple_of(lax.axis_index("heads") * width, 128)
     part = jnp.dot(att_ref[...], w_ref[:, pl.ds(first, width)], preferred_element_type=F32)
     out_ref[...] = part + stream_ref[...].astype(F32) + b_ref[...].reshape(1, width)
 
@@ -184,8 +184,6 @@
     group_size = full // GROUPS
     n = lax.axis_size("patch")
     swap = [(0, 1), (1, 0)]
-    h = lax.axis_index("heads").astype(jnp.int32).reshape(1)
-    smem = {0: pltpu.SMEM}
 
     kv_own = stale_kv.reshape(2 * tok, width)
     partner = lambda k: [(i, i ^ k) for i in range(n)]
@@ -228,12 +226,10 @@
         count = float(tok * n) / 2.0
 
     stream = call(
-        functools.partial(in_kernel, count, group_size), sds((tok, width), BF), 9, spaces=smem, flops=COVER
-    )(h, stat, stat_x, hidden_in, other, gb, gb_other, b_in, w_in)
+        functools.partial(in_kernel, count, group_size), sds((tok, width), BF), 8, flops=COVER
+    )(stat, stat_x, hidden_in, other, gb, gb_other, b_in, w_in)
     stream_other = move(stream, 0)
-    qkv = call(qkv_kernel, sds((3, tok, width), BF), 6, spaces=smem, flops=COVER)(
-        h, stream, stream_other, ln_gain, ln_bias, w_qkv
-    )
+    qkv = call(qkv_kernel, sds((3, tok, width), BF), 5, flops=COVER)(stream, stream_other, ln_gain, ln_bias, w_qkv)
     n_keys = n * tok
     if not direct:
         kv_all = lax.all_gather(stale_kv, "patch", axis=1, tiled=True)
@@ -243,13 +239,12 @@
     attended, send = call(
         functools.partial(attn_kernel, sources),
         (sds((tok, width), BF), sds((tok, width), F32)),
-        3 + len(strips),
+        2 + len(strips),
         scratch=[VMEM((n_keys, width), BF), VMEM((n_keys, width), BF)],
         extra=4 * n_keys * width + 16 * 2 * tok * n_keys,
-        spaces=smem,
-    )(h, qkv, *strips, w_out)
+    )(qkv, *strips, w_out)
     received = move(send, 0)
-    mine = call(own_kernel, sds((tok, width), F32), 5, spaces=smem)(h, attended, stream, b_out, w_out)
+    mine = call(own_kernel, sds((tok, width), F32), 4)(attended, stream, b_out, w_out)
     return mine + received
 
 

time: 35.7 us -> 35.7 us (level)
  local copies, waits for them, and re-layouts: 2.43 us -> 0.05 us
  waiting for transfers between devices: 18.2 us -> 20.5 us
    unnamed x22 -> x24, local copies, waits for them, and re-layouts: 2.43 us -> 0.05 us
    ppermute x7, waiting for transfers between devices: 14.9 us -> 17.2 us  [move(): lax.ppermute(x, 'patch', partner(k))]
  transfers between devices with their start and end apart: 11 -> 11, of which waited for: 9 -> 10; matrix products, arithmetic and copies ran while one was open for 0% -> 0% of each run, Pallas kernels for 4% -> 4%
where the time goes in v1:
time: 35.7 us; the launch traced here: 35.5 us
  waiting for transfers between devices  20.5 us (57%)
  starting transfers between devices  10.8 us (30%)
  Pallas kernels  3.49 us (10%)
  other arithmetic  0.65 us (2%)
    ppermute x7, waiting for transfers between devices, move(): lax.ppermute(x, 'patch', partner(k))  17.2 us
    ppermute x7, starting transfers between devices, move(): lax.ppermute(x, 'patch', partner(k))  9.97 us
    ppermute x4, waiting for transfers between devices, move(): lax.ppermute(x, 'heads', swap)  3.22 us
    pallas_call x1, Pallas kernels, body(): call(functools.partial(attn_kernel, sources), (sds((tok, width), BF), sds...  1.49 us
    pallas_call x1, Pallas kernels, body(): call(qkv_kernel, sds((3, tok, width), BF), 5, flops=COVER)  0.99 us
    ppermute x4, starting transfers between devices, move(): lax.ppermute(x, 'heads', swap)  0.78 us
  transfers between devices with their start and end apart: 11, of which 10 were waited for; matrix products, arithmetic and copies ran while one was open for 0% of the time, Pallas kernels for 4%

profile of v1, /device:TPU:0, one launch (start us, length us, event | category | flops | bytes accessed | tf_op | source)
XLA Modules:
  0.0 35.5 jit_solution(8087589170935537909)
XLA Ops:
  0.0 0.0 copy-start.4
  0.0 0.0 copy-start.3
  0.0 0.0 copy-start.8
  0.0 0.0 copy-start.7
  0.0 0.6 %collective-permute-start = (bf16[32,640]{1,0:T(8,128)(2,1)}, bf16[32,640]{1,0:T(8,128)(2,1)S(1)}, u32[]{:S(2)}, u32[]{:S(2)}) collective-permute-start(bf16[32,640]{1,0:T(8,128)(2,1)} %own_ref.3), channel_id=1, source_target_pairs={{0,1},{1,0},{2,3},{3,2},{4,5},{5,4},{6,7},{7,6},{8,9},{9,8},{10,11... | collective-permute-start | bytes 122888 | tf_op jit(solution)/shard_map/ppermute | solution.py:192
  0.6 1.1 %collective-permute-done.other_ref = bf16[32,640]{1,0:T(8,128)(2,1)S(1)} collective-permute-done((bf16[32,640]{1,0:T(8,128)(2,1)}, bf16[32,640]{1,0:T(8,128)(2,1)S(1)}, u32[]{:S(2)}, u32[]{:S(2)}) %collective-permute-start) | collective-permute-done | bytes 40992 | tf_op jit(solution)/shard_map/ppermute | solution.py:192
  1.7 0.0 copy-done.4
  1.7 0.0 copy-done.3
  1.7 0.0 copy-done.8
  1.7 0.0 copy-done.7
  1.7 0.1 shard_map.110
  1.8 0.0 copy-start.2
  1.8 0.0 copy-start.9
  1.8 3.0 %collective-permute-start.3 = (bf16[80,640]{1,0:T(8,128)(2,1)S(1)}, bf16[80,640]{1,0:T(8,128)(2,1)S(1)}, u32[]{:S(2)}, u32[]{:S(2)}) collective-permute-start(bf16[80,640]{1,0:T(8,128)(2,1)S(1)} %get-tuple-element.11.refs_0_), channel_id=1, source_target_pairs={{0,4},{2,6},{4,0},{6,2},{8,12},{10,14},{12,8},{14,10},{1,5},{3,7},... | collective-permute-start | bytes 307208 | tf_op jit(solution)/shard_map/ppermute | solution.py:192
  4.8 2.5 %collective-permute-start.2 = (bf16[80,640]{1,0:T(8,128)(2,1)S(1)}, bf16[80,640]{1,0:T(8,128)(2,1)S(1)}, u32[]{:S(2)}, u32[]{:S(2)}) collective-permute-start(bf16[80,640]{1,0:T(8,128)(2,1)S(1)} %get-tuple-element.11.refs_0_), channel_id=1, source_target_pairs={{0,12},{2,14},{4,8},{6,10},{8,4},{10,6},{12,0},{14,2},{1,13},{3,15... | collective-permute-start | bytes 307208 | tf_op jit(solution)/shard_map/ppermute | solution.py:192
  7.2 0.1 collective-permute-start.1
  7.4 0.6 %collective-permute-done.3.refs_3_.refs_1_ = bf16[80,640]{1,0:T(8,128)(2,1)S(1)} collective-permute-done((bf16[80,640]{1,0:T(8,128)(2,1)S(1)}, bf16[80,640]{1,0:T(8,128)(2,1)S(1)}, u32[]{:S(2)}, u32[]{:S(2)}) %collective-permute-start.3) | collective-permute-done | bytes 102432 | tf_op jit(solution)/shard_map/ppermute | solution.py:192
  8.0 5.3 %collective-permute-done.2.refs_2_ = bf16[80,640]{1,0:T(8,128)(2,1)S(1)} collective-permute-done((bf16[80,640]{1,0:T(8,128)(2,1)S(1)}, bf16[80,640]{1,0:T(8,128)(2,1)S(1)}, u32[]{:S(2)}, u32[]{:S(2)}) %collective-permute-start.2) | collective-permute-done | bytes 102432 | tf_op jit(solution)/shard_map/ppermute | solution.py:192
  13.3 3.6 %collective-permute-done.1.refs_1_ = bf16[80,640]{1,0:T(8,128)(2,1)S(1)} collective-permute-done((bf16[80,640]{1,0:T(8,128)(2,1)S(1)}, bf16[80,640]{1,0:T(8,128)(2,1)S(1)}, u32[]{:S(2)}, u32[]{:S(2)}) %collective-permute-start.1) | collective-permute-done | bytes 102432 | tf_op jit(solution)/shard_map/ppermute | solution.py:192
  16.9 0.1 shard_map.111
  16.9 1.6 %collective-permute-start.4 = (f32[8,640]{1,0:T(8,128)S(1)}, f32[8,640]{1,0:T(8,128)S(1)}, u32[]{:S(2)}, u32[]{:S(2)}) collective-permute-start(f32[8,640]{1,0:T(8,128)S(1)} %get-tuple-element.12.st_a), channel_id=1, source_target_pairs={{0,2},{2,0},{4,6},{6,4},{8,10},{10,8},{12,14},{14,12},{1,3},{3,1},... | collective-permute-start | bytes 61448 | tf_op jit(solution)/shard_map/ppermute | solution.py:192
  18.5 0.1 collective-permute-start.5
  18.6 1.2 %collective-permute-done.5.gb2_ref = f32[2,640]{1,0:T(2,128)S(1)} collective-permute-done((f32[2,640]{1,0:T(2,128)S(1)}, f32[2,640]{1,0:T(2,128)S(1)}, u32[]{:S(2)}, u32[]{:S(2)}) %collective-permute-start.5) | collective-permute-done | bytes 5152 | tf_op jit(solution)/shard_map/ppermute | solution.py:192
  19.7 1.0 %collective-permute-done.4.st_b = f32[8,640]{1,0:T(8,128)S(1)} collective-permute-done((f32[8,640]{1,0:T(8,128)S(1)}, f32[8,640]{1,0:T(8,128)S(1)}, u32[]{:S(2)}, u32[]{:S(2)}) %collective-permute-start.4) | collective-permute-done | bytes 20512 | tf_op jit(solution)/shard_map/ppermute | solution.py:192
  20.8 0.0 copy-done.2
  20.8 0.0 copy-done.9
  20.8 0.6 %shard_map.112.own_ref.stream_ref = bf16[32,640]{1,0:T(8,128)(2,1)S(1)} custom-call(f32[8,640]{1,0:T(8,128)S(1)} %get-tuple-element.12.st_a, f32[8,640]{1,0:T(8,128)S(1)} %collective-permute-done.4.st_b, bf16[32,640]{1,0:T(8,128)(2,1)S(1)} %copy-done.4, bf16[32,640]{1,0:T(8,128)(2,1)S(1)} %collective-permute-done.other_ref, ...), custom_call_target="tpu_custom_call" | custom-call | flops 10000000000 | bytes 131072 | tf_op jit(solution)/shard_map/pallas_call | solution.py:228
  21.4 0.1 collective-permute-start.6
  21.5 0.8 %collective-permute-start.8 = (bf16[64,640]{1,0:T(8,128)(2,1)S(1)}, bf16[64,640]{1,0:T(8,128)(2,1)S(1)}, u32[]{:S(2)}, u32[]{:S(2)}) collective-permute-start(bf16[64,640]{1,0:T(8,128)(2,1)S(1)} %bitcast.4), channel_id=1, source_target_pairs={{0,6},{2,4},{4,2},{6,0},{8,14},{10,12},{12,10},{14,8},{1,7},{3,5},... | collective-permute-start | bytes 245768 | tf_op jit(solution)/shard_map/ppermute | solution.py:192
  22.3 0.8 %collective-permute-start.7 = (bf16[64,640]{1,0:T(8,128)(2,1)S(1)}, bf16[64,640]{1,0:T(8,128)(2,1)S(1)}, u32[]{:S(2)}, u32[]{:S(2)}) collective-permute-start(bf16[64,640]{1,0:T(8,128)(2,1)S(1)} %bitcast.5), channel_id=1, source_target_pairs={{0,2},{2,0},{4,6},{6,4},{8,10},{10,8},{12,14},{14,12},{1,3},{3,1},... | collective-permute-start | bytes 245768 | tf_op jit(solution)/shard_map/ppermute | solution.py:192
  23.1 1.2 %collective-permute-start.9 = (bf16[128,640]{1,0:T(8,128)(2,1)S(1)}, bf16[128,640]{1,0:T(8,128)(2,1)S(1)}, u32[]{:S(2)}, u32[]{:S(2)}) collective-permute-start(bf16[128,640]{1,0:T(8,128)(2,1)S(1)} %get-tuple-element.14.refs_3_), channel_id=1, source_target_pairs={{0,2},{2,0},{4,6},{6,4},{8,10},{10,8},{12,14},{14,12},{1,3},{3,1},... | collective-permute-start | bytes 491528 | tf_op jit(solution)/shard_map/ppermute | solution.py:192
  24.3 0.0 collective-permute-done.6.other_ref
  24.3 0.0 slice-done
  24.3 0.0 slice-done.1
  24.3 0.0 copy-done.5
  24.3 0.0 copy-done.6
  24.3 1.0 %shard_map.113.qkv_ref = bf16[3,32,640]{2,1,0:T(8,128)(2,1)S(1)} custom-call(bf16[32,640]{1,0:T(8,128)(2,1)S(1)} %shard_map.112.own_ref.stream_ref, bf16[32,640]{1,0:T(8,128)(2,1)S(1)} %collective-permute-done.6.other_ref, f32[1280]{0:T(1024)S(1)} %copy-done.5, f32[1280]{0:T(1024)S(1)} %copy-done.6, bf16[3,1280,640]{2,1,0:T(8,128)(2,1)S(1)} %bitcast.2), custom_call_target="tpu_custom_call" | custom-call | flops 10000000000 | bytes 131072 | tf_op jit(solution)/shard_map/pallas_call | solution.py:232
  25.3 0.0 copy-start.1
  25.3 1.9 %collective-permute-done.8.refs_2_ = bf16[64,640]{1,0:T(8,128)(2,1)S(1)} collective-permute-done((bf16[64,640]{1,0:T(8,128)(2,1)S(1)}, bf16[64,640]{1,0:T(8,128)(2,1)S(1)}, u32[]{:S(2)}, u32[]{:S(2)}) %collective-permute-start.8) | collective-permute-done | bytes 81952 | tf_op jit(solution)/shard_map/ppermute | solution.py:192
  27.3 1.7 %collective-permute-done.7.refs_0_ = bf16[64,640]{1,0:T(8,128)(2,1)S(1)} collective-permute-done((bf16[64,640]{1,0:T(8,128)(2,1)S(1)}, bf16[64,640]{1,0:T(8,128)(2,1)S(1)}, u32[]{:S(2)}, u32[]{:S(2)}) %collective-permute-start.7) | collective-permute-done | bytes 81952 | tf_op jit(solution)/shard_map/ppermute | solution.py:192
  29.0 3.0 %collective-permute-done.9.refs_4_ = bf16[128,640]{1,0:T(8,128)(2,1)S(1)} collective-permute-done((bf16[128,640]{1,0:T(8,128)(2,1)S(1)}, bf16[128,640]{1,0:T(8,128)(2,1)S(1)}, u32[]{:S(2)}, u32[]{:S(2)}) %collective-permute-start.9) | collective-permute-done | bytes 163872 | tf_op jit(solution)/shard_map/ppermute | solution.py:192
  32.0 0.0 copy-done
  32.0 1.5 %shard_map.114 = (bf16[32,640]{1,0:T(8,128)(2,1)S(1)}, f32[32,640]{1,0:T(8,128)S(1)}) custom-call(bf16[3,32,640]{2,1,0:T(8,128)(2,1)S(1)} %shard_map.113.qkv_ref, bf16[64,640]{1,0:T(8,128)(2,1)S(1)} %collective-permute-done.7.refs_0_, bf16[80,640]{1,0:T(8,128)(2,1)S(1)} %collective-permute-done.3.refs_3_.refs_1_, ...), custom_call_target="tpu_custom_call" | custom-call | bytes 131072 | tf_op jit(solution)/shard_map/pallas_call | solution.py:239
  33.5 0.1 collective-permute-start.10
  33.6 0.0 copy-done.1
  33.6 0.3 shard_map.115
  33.9 1.0 %collective-permute-done.10 = f32[32,640]{1,0:T(8,128)S(1)} collective-permute-done((f32[32,640]{1,0:T(8,128)S(1)}, f32[32,640]{1,0:T(8,128)S(1)}, u32[]{:S(2)}, u32[]{:S(2)}) %collective-permute-start.10) | collective-permute-done | bytes 81952 | tf_op jit(solution)/shard_map/ppermute | solution.py:192
  34.9 0.6 %add.3 = f32[32,640]{1,0:T(8,128)} add(f32[32,640]{1,0:T(8,128)S(1)} %shard_map.115, f32[32,640]{1,0:T(8,128)S(1)} %collective-permute-done.10) | non-fusion elementwise | flops 20480 | bytes 245760 | tf_op jit(solution)/shard_map/add | solution.py:248
  (7 shorter events, 0.0 us)
Async XLA Ops:
  0.0 1.7 %copy-start.4 = (bf16[32,640]{1,0:T(8,128)(2,1)S(1)}, bf16[32,640]{1,0:T(8,128)(2,1)}, u32[]{:S(2)}) copy-start(bf16[32,640]{1,0:T(8,128)(2,1)} %own_ref.3) | copy-start | bytes 122884
  0.0 1.7 %copy-start.3 = (bf16[2,32,640]{2,1,0:T(8,128)(2,1)S(1)}, bf16[2,32,640]{2,1,0:T(8,128)(2,1)}, u32[]{:S(2)}) copy-start(bf16[2,32,640]{2,1,0:T(8,128)(2,1)} %param.19) | copy-start | bytes 245764
  0.0 1.7 %copy-start.8 = (f32[640]{0:T(1024)S(1)}, f32[640]{0:T(1024)}, u32[]{:S(2)}) copy-start(f32[640]{0:T(1024)} %bias_ref.2) | copy-start | bytes 7684
  0.0 1.7 %copy-start.7 = (f32[640]{0:T(1024)S(1)}, f32[640]{0:T(1024)}, u32[]{:S(2)}) copy-start(f32[640]{0:T(1024)} %gain_ref.2) | copy-start | bytes 7684
  0.0 1.6 %collective-permute-start = (bf16[32,640]{1,0:T(8,128)(2,1)}, bf16[32,640]{1,0:T(8,128)(2,1)S(1)}, u32[]{:S(2)}, u32[]{:S(2)}) collective-permute-start(bf16[32,640]{1,0:T(8,128)(2,1)} %own_ref.3), channel_id=1, source_target_pairs={{0,1},{1,0},{2,3},{3,2},{4,5},{5,4},{6,7},{7,6},{8,9},{9,8},{10,11... | collective-permute-start | bytes 122888 | tf_op jit(solution)/shard_map/ppermute | solution.py:192
  1.8 19.0 %copy-start.2 = (bf16[1280,640]{1,0:T(8,128)(2,1)S(1)}, bf16[1280,640]{1,0:T(8,128)(2,1)}, u32[]{:S(2)}) copy-start(bf16[1280,640]{1,0:T(8,128)(2,1)} %w_ref.3) | copy-start | bytes 4915204
  1.8 19.0 %copy-start.9 = (f32[640]{0:T(1024)S(1)}, f32[640]{0:T(1024)}, u32[]{:S(2)}) copy-start(f32[640]{0:T(1024)} %b_ref.2) | copy-start | bytes 7684
  1.8 6.2 %collective-permute-start.3 = (bf16[80,640]{1,0:T(8,128)(2,1)S(1)}, bf16[80,640]{1,0:T(8,128)(2,1)S(1)}, u32[]{:S(2)}, u32[]{:S(2)}) collective-permute-start(bf16[80,640]{1,0:T(8,128)(2,1)S(1)} %get-tuple-element.11.refs_0_), channel_id=1, source_target_pairs={{0,4},{2,6},{4,0},{6,2},{8,12},{10,14},{12,8},{14,10},{1,5},{3,7},... | collective-permute-start | bytes 307208 | tf_op jit(solution)/shard_map/ppermute | solution.py:192
  4.8 8.5 %collective-permute-start.2 = (bf16[80,640]{1,0:T(8,128)(2,1)S(1)}, bf16[80,640]{1,0:T(8,128)(2,1)S(1)}, u32[]{:S(2)}, u32[]{:S(2)}) collective-permute-start(bf16[80,640]{1,0:T(8,128)(2,1)S(1)} %get-tuple-element.11.refs_0_), channel_id=1, source_target_pairs={{0,12},{2,14},{4,8},{6,10},{8,4},{10,6},{12,0},{14,2},{1,13},{3,15... | collective-permute-start | bytes 307208 | tf_op jit(solution)/shard_map/ppermute | solution.py:192
  7.2 9.6 %collective-permute-start.1 = (bf16[80,640]{1,0:T(8,128)(2,1)S(1)}, bf16[80,640]{1,0:T(8,128)(2,1)S(1)}, u32[]{:S(2)}, u32[]{:S(2)}) collective-permute-start(bf16[80,640]{1,0:T(8,128)(2,1)S(1)} %get-tuple-element.11.refs_0_), channel_id=1, source_target_pairs={{0,8},{2,10},{4,12},{6,14},{8,0},{10,2},{12,4},{14,6},{1,9},{3,11}... | collective-permute-start | bytes 307208 | tf_op jit(solution)/shard_map/ppermute | solution.py:192
  16.9 3.8 %collective-permute-start.4 = (f32[8,640]{1,0:T(8,128)S(1)}, f32[8,640]{1,0:T(8,128)S(1)}, u32[]{:S(2)}, u32[]{:S(2)}) collective-permute-start(f32[8,640]{1,0:T(8,128)S(1)} %get-tuple-element.12.st_a), channel_id=1, source_target_pairs={{0,2},{2,0},{4,6},{6,4},{8,10},{10,8},{12,14},{14,12},{1,3},{3,1},... | collective-permute-start | bytes 61448 | tf_op jit(solution)/shard_map/ppermute | solution.py:192
  18.5 5.8 %slice-start = ((s8[4915200]{0:T(1024)(128)(4,1)}), s8[4194304]{0:T(1024)(128)(4,1)S(1)}, s32[]{:S(2)}) async-start(s8[4915200]{0:T(1024)(128)(4,1)} %bitcast.1), calls=%async_computation | async-start | bytes 8388608
  18.5 5.8 %slice-start.1 = ((s8[4915200]{0:T(1024)(128)(4,1)}), s8[720896]{0:T(1024)(128)(4,1)S(1)}, s32[]{:S(2)}) async-start(s8[4915200]{0:T(1024)(128)(4,1)} %bitcast.1), calls=%async_computation.1 | async-start | bytes 1441792
  18.5 5.8 %copy-start.5 = (f32[1280]{0:T(1024)S(1)}, f32[1280]{0:T(1024)}, u32[]{:S(2)}) copy-start(f32[1280]{0:T(1024)} %gain_ref.3) | copy-start | bytes 15364
  18.5 5.8 %copy-start.6 = (f32[1280]{0:T(1024)S(1)}, f32[1280]{0:T(1024)}, u32[]{:S(2)}) copy-start(f32[1280]{0:T(1024)} %bias_ref.3) | copy-start | bytes 15364
  18.5 1.2 %collective-permute-start.5 = (f32[2,640]{1,0:T(2,128)S(1)}, f32[2,640]{1,0:T(2,128)S(1)}, u32[]{:S(2)}, u32[]{:S(2)}) collective-permute-start(f32[2,640]{1,0:T(2,128)S(1)} %get-tuple-element.13.gb_ref), channel_id=1, source_target_pairs={{0,1},{1,0},{2,3},{3,2},{4,5},{5,4},{6,7},{7,6},{8,9},{9,8},{10,11... | collective-permute-start | bytes 15368 | tf_op jit(solution)/shard_map/ppermute | solution.py:192
  21.4 2.9 %collective-permute-start.6 = (bf16[32,640]{1,0:T(8,128)(2,1)S(1)}, bf16[32,640]{1,0:T(8,128)(2,1)S(1)}, u32[]{:S(2)}, u32[]{:S(2)}) collective-permute-start(bf16[32,640]{1,0:T(8,128)(2,1)S(1)} %shard_map.112.own_ref.stream_ref), channel_id=1, source_target_pairs={{0,1},{1,0},{2,3},{3,2},{4,5},{5,4},{6,7},{7,6},{8,9},{9,8},{10,11... | collective-permute-start | bytes 122888 | tf_op jit(solution)/shard_map/ppermute | solution.py:192
  21.5 5.8 %collective-permute-start.8 = (bf16[64,640]{1,0:T(8,128)(2,1)S(1)}, bf16[64,640]{1,0:T(8,128)(2,1)S(1)}, u32[]{:S(2)}, u32[]{:S(2)}) collective-permute-start(bf16[64,640]{1,0:T(8,128)(2,1)S(1)} %bitcast.4), channel_id=1, source_target_pairs={{0,6},{2,4},{4,2},{6,0},{8,14},{10,12},{12,10},{14,8},{1,7},{3,5},... | collective-permute-start | bytes 245768 | tf_op jit(solution)/shard_map/ppermute | solution.py:192
  22.3 6.8 %collective-permute-start.7 = (bf16[64,640]{1,0:T(8,128)(2,1)S(1)}, bf16[64,640]{1,0:T(8,128)(2,1)S(1)}, u32[]{:S(2)}, u32[]{:S(2)}) collective-permute-start(bf16[64,640]{1,0:T(8,128)(2,1)S(1)} %bitcast.5), channel_id=1, source_target_pairs={{0,2},{2,0},{4,6},{6,4},{8,10},{10,8},{12,14},{14,12},{1,3},{3,1},... | collective-permute-start | bytes 245768 | tf_op jit(solution)/shard_map/ppermute | solution.py:192
  23.1 9.0 %copy-start = (bf16[640,1280]{1,0:T(8,128)(2,1)S(1)}, bf16[640,1280]{1,0:T(8,128)(2,1)}, u32[]{:S(2)}) copy-start(bf16[640,1280]{1,0:T(8,128)(2,1)} %w_ref.5) | copy-start | bytes 4915204
  23.1 8.9 %collective-permute-start.9 = (bf16[128,640]{1,0:T(8,128)(2,1)S(1)}, bf16[128,640]{1,0:T(8,128)(2,1)S(1)}, u32[]{:S(2)}, u32[]{:S(2)}) collective-permute-start(bf16[128,640]{1,0:T(8,128)(2,1)S(1)} %get-tuple-element.14.refs_3_), channel_id=1, source_target_pairs={{0,2},{2,0},{4,6},{6,4},{8,10},{10,8},{12,14},{14,12},{1,3},{3,1},... | collective-permute-start | bytes 491528 | tf_op jit(solution)/shard_map/ppermute | solution.py:192
  25.3 8.3 %copy-start.1 = (f32[640]{0:T(1024)S(1)}, f32[640]{0:T(1024)}, u32[]{:S(2)}) copy-start(f32[640]{0:T(1024)} %b_ref.3) | copy-start | bytes 7684
  33.5 1.3 %collective-permute-start.10 = (f32[32,640]{1,0:T(8,128)S(1)}, f32[32,640]{1,0:T(8,128)S(1)}, u32[]{:S(2)}, u32[]{:S(2)}) collective-permute-start(f32[32,640]{1,0:T(8,128)S(1)} %get-tuple-element.16), channel_id=1, source_target_pairs={{0,1},{1,0},{2,3},{3,2},{4,5},{5,4},{6,7},{7,6},{8,9},{9,8},{10,11... | collective-permute-start | bytes 245768 | tf_op jit(solution)/shard_map/ppermute | solution.py:192
